TPU v7x, 32 devices: a whole 2x2x4 slice. The times are simulated.
32 devices in a mesh: seg: 2 (over y), ch: 16 (over z, x, core).
Axes of the slice: x: 2, y: 2, z: 4, core: 2. Of those that a mesh axis runs over, the one named last changes fastest.
Arguments:
- strain: float32 [2, 1024, 2048], P('seg', 'ch')
- ref_local: int32 [4, 16], replicated, may hold values from 0 to 127, as said below
- owners: int32 [4], replicated, may hold values from 0 to 15, as said below
Outputs:
- toeplitz_blocks: float32 [64, 2048, 64], P('seg', 'ch')
Inputs may be any that keep to these rules, and one draw needn't show every extreme that they name: `ref_local`: each row holds 16 distinct offsets; the first row holds 127. `owners`: the 4 entries are distinct, and one of them is 15.
All inputs are finite; a program needn't handle non-finite values.
Results may differ from a plain program's by a relative error of at most 0.0029.
Values may be sent and summed in bfloat16 or wider, within the bound.
A program may use at most 64 MiB of HBM per device.

v0:
```python
import jax
import jax.numpy as jnp
from jax import lax
from jax.sharding import PartitionSpec as P

L = 64


def spread_2(block, axis, holder):
    block = jnp.where(lax.axis_index(axis) == holder, block, jnp.zeros_like(block))
    return lax.psum(block, axis)


def detrend_cols(series):
    n_total = series.shape[0]
    mid_time = (n_total - 1) / 2.0
    spread = n_total * (n_total * n_total - 1) / 12.0
    centred = (jnp.arange(n_total, dtype=jnp.float32) - mid_time)[:, None]
    level_val = jnp.sum(series, axis=0) / n_total
    slope_val = jnp.sum(centred * series, axis=0) / spread
    return (series - level_val - slope_val * centred).astype(jnp.bfloat16)


def owner_panels(detrended, ref_local, owners):
    pieces = []
    for panel_id in range(ref_local.shape[0]):
        own_cols = jnp.take(detrended, ref_local[panel_id], axis=1)
        pieces.append(spread_2(own_cols, "ch", owners[panel_id]))
    return jnp.concatenate(pieces, axis=1)


def per_device(strain, ref_local, owners):
    my_rows = strain[0]
    s_dev, chans = my_rows.shape
    n_ch = lax.axis_size("ch")
    n_seg = lax.axis_size("seg")
    n_total = s_dev * n_ch
    c_dev = chans // n_ch
    series = lax.all_to_all(my_rows, "ch", split_axis=1, concat_axis=0, tiled=True)
    detrended = detrend_cols(series)
    panels = owner_panels(detrended, ref_local, owners)
    width_ref = panels.shape[1]
    padded = jnp.concatenate([detrended, jnp.zeros((L, c_dev), jnp.bfloat16)], axis=0)
    blk_rows = min(512, n_total)
    n_blocks = n_total // blk_rows
    lag_dev = L // n_seg
    lag_count = lax.axis_size("seg") * lag_dev

    def add_block(blk_idx, running):
        blk_start = blk_idx * blk_rows
        window = lax.dynamic_slice_in_dim(padded, blk_start, blk_rows + lag_count - 1, 0)
        lagged = jnp.concatenate(
            [window[lag_off : lag_off + blk_rows] for lag_off in range(lag_count)], axis=1
        )
        ref_block = lax.dynamic_slice_in_dim(panels, blk_start, blk_rows, 0)
        return running + lax.dot_general(
            lagged, ref_block, (((0,), (0,)), ((), ())), preferred_element_type=jnp.float32
        )

    start_acc = jnp.zeros((lag_count * c_dev, width_ref), jnp.float32)
    running = lax.fori_loop(0, n_blocks, add_block, start_acc)
    summed = lax.psum_scatter(
        running.reshape(lag_count, c_dev, width_ref), "seg", scatter_dimension=0, tiled=True
    )
    lag_ids = (lax.axis_index("seg") * lag_dev + jnp.arange(lag_dev, dtype=jnp.int32)).astype(
        jnp.float32
    )
    return summed / (n_seg * (n_total - lag_ids))[:, None, None]


def solution(mesh):
    in_specs = (P("seg", "ch", None), P(), P())
    out_specs = P("seg", "ch", None)
    return jax.shard_map(
        per_device, mesh=mesh, in_specs=in_specs, out_specs=out_specs, check_vma=False
    )
```

profile of v0, /device:TPU:0, one launch (start us, length us, event | category | flops | bytes accessed | tf_op | source)
XLA Modules:
  0.0 272.1 jit_solution(4993539267196957720)
XLA Ops:
  6.5 1.1 copy.23
  7.7 1.0 copy.16
  8.6 7.4 %all-to-all-start = ((f32[64,16,128]{2,0,1:T(8,128)}), f32[64,16,128]{2,0,1:T(8,128)S(1)}, u32[]{:S(2)}, u32[]{:S(2)}) async-start(f32[64,16,128]{2,0,1:T(8,128)} %copy.16), calls=%async_computation | async-start | bytes 1048576 | tf_op jit(solution)/shard_map/all_to_all | solution.py:39
  16.1 1.5 fusion.3
  20.0 0.8 compare_and_fusion.3
  20.9 9.4 %all-to-all-done = f32[64,16,128]{2,0,1:T(8,128)S(1)} async-done(((f32[64,16,128]{2,0,1:T(8,128)}), f32[64,16,128]{2,0,1:T(8,128)S(1)}, u32[]{:S(2)}, u32[]{:S(2)}) %all-to-all-start) | async-done | bytes 524320 | tf_op jit(solution)/shard_map/all_to_all | solution.py:39
  36.4 88.2 %all-reduce.4.cloned.1.call-done = (bf16[1024,16]{0,1:T(8,128)(2,1)}, bf16[1024,16]{0,1:T(8,128)(2,1)}, bf16[1024,16]{0,1:T(8,128)(2,1)}, bf16[1024,16]{0,1:T(8,128)(2,1)}) async-done(((bf16[1024,16]{0,1:T(8,128)(2,1)}, bf16[1024,16]{0,1:T(8,128)(2,1)}, bf16[1024,16]{0,1:T(8,128)(2,1)}, bf16[1024,16]{0,1:T(8,128)(2,1)}), (bf16[1024,16]{0,1:T(8,128)(2,1)}, bf16[1024,16]{0,1:T(8,128)(2,1)}, ...) | async-done | bytes 131088 | tf_op jit(solution)/shard_map/psum | solution.py:11
  124.6 0.8 pad_maximum_fusion
  125.4 101.3 %while.14 = (s32[]{:T(128)}, f32[8192,64]{0,1:T(8,128)S(1)}, bf16[1088,128]{1,0:T(8,128)(2,1)S(1)}, bf16[1024,64]{0,1:T(8,128)(2,1)S(1)}, s32[]{:T(128)}, /*inde...) while((s32[]{:T(128)}, f32[8192,64]{0,1:T(8,128)S(1)}, ...), condition=%wide.region_7.9_spmd.clone, body=%wide.region_6.8_spmd.clone.sunk | while | flops 537919552 | bytes 29427356 | solution.py:61
  135.3 0.8 constant_dynamic-update-slice_fusion.142
  143.1 0.7 constant_dynamic-update-slice_fusion.153
  146.7 0.8 constant_dynamic-update-slice_fusion.158
  150.3 0.8 constant_dynamic-update-slice_fusion.163
  163.1 0.8 constant_dynamic-update-slice_fusion.181
  170.9 5.2 %convolution_add_fusion.2 = f32[8192,64]{0,1:T(8,128)S(1)} fusion(bf16[512,8192]{1,0:T(8,128)(2,1)} %constant_dynamic-update-slice_fusion.191, f32[8192,64]{0,1:T(8,128)S(1)} %get-tuple-element.251, pred[]{:T(512)S(6)} %compare.4, bf16[1024,64]{0,1:T(8,128)(2,1)S(1)} %get-tuple-element.325, s32[]{:T(128)S(6)} %select_n.98), kind=kOutput, calls=%fused_computation.4.clone.1 | convolution fusion | flops 537919488 | bytes 12648453 | tf_op jit(solution)/shard_map/while/body/eval_jaxpr/dot_general | solution.py:56
  185.9 0.8 constant_dynamic-update-slice_fusion.142
  197.3 0.8 constant_dynamic-update-slice_fusion.158
  200.9 0.8 constant_dynamic-update-slice_fusion.163
  213.7 0.8 constant_dynamic-update-slice_fusion.181
  221.5 5.2 %convolution_add_fusion.2 = f32[8192,64]{0,1:T(8,128)S(1)} fusion(bf16[512,8192]{1,0:T(8,128)(2,1)} %constant_dynamic-update-slice_fusion.191, f32[8192,64]{0,1:T(8,128)S(1)} %get-tuple-element.251, pred[]{:T(512)S(6)} %compare.4, bf16[1024,64]{0,1:T(8,128)(2,1)S(1)} %get-tuple-element.325, s32[]{:T(128)S(6)} %select_n.98), kind=kOutput, calls=%fused_computation.4.clone.1 | convolution fusion | flops 537919488 | bytes 12648453 | tf_op jit(solution)/shard_map/while/body/eval_jaxpr/dot_general | solution.py:56
  226.7 1.7 copy.24
  228.5 33.8 %reduce-scatter.2.cloned.1.call-done = f32[32,128,64]{1,0,2:T(8,128)} async-done(((f32[64,128,64]{1,0,2:T(8,128)}), f32[32,128,64]{1,0,2:T(8,128)}) %reduce-scatter.2.cloned.1.call-update) | async-done | bytes 1048592 | tf_op jit(solution)/shard_map/reduce_scatter | solution.py:62
  262.3 1.4 broadcast_divide_fusion
  263.7 1.6 copy.20
  (144 shorter events, 90.2 us)
Async XLA Ops:
  8.6 21.7 %all-to-all-start = ((f32[64,16,128]{2,0,1:T(8,128)}), f32[64,16,128]{2,0,1:T(8,128)S(1)}, u32[]{:S(2)}, u32[]{:S(2)}) async-start(f32[64,16,128]{2,0,1:T(8,128)} %copy.16), calls=%async_computation | async-start | bytes 1048576 | tf_op jit(solution)/shard_map/all_to_all | solution.py:39
  16.0 108.6 %all-reduce.4.cloned.1.call-start = ((), (), s32[]{:S(2)}) async-start(), calls=%async_computation.3 | async-start | bytes 262144 | tf_op jit(solution)/shard_map/psum | solution.py:11
  36.2 226.1 %reduce-scatter.2.cloned.1.call-start = ((), (), s32[]{:S(2)}) async-start(), calls=%async_computation.2 | async-start | bytes 3145728 | tf_op jit(solution)/shard_map/reduce_scatter | solution.py:62
Sparse Core Ops, SparseCore 0:
  36.3 88.2 all-reduce.3
  228.6 33.6 reduce-scatter.1
where the time goes:
time: 273 us; the launch traced here: 272 us
  waiting for transfers between devices  131 us (48%)
  local copies, waits for them, and re-layouts  100 us (37%)
  between operations  16 us (6%)
  matrix products  10.4 us (4%)
  starting transfers between devices  7.47 us (3%)
  other arithmetic  6.38 us (2%)
    while x126, local copies, waits for them, and re-layouts  89.4 us
    psum x1, waiting for transfers between devices, spread_2(): return lax.psum(block, axis)  88.2 us
    reduce_scatter x1, waiting for transfers between devices, per_device(): lax.psum_scatter(running.reshape(lag_count, c_dev, width_ref), 'seg', sca...  33.8 us
    dot_general x2, matrix products, add_block(): lax.dot_general(lagged, ref_block, (((0,), (0,)), ((), ())), preferred_el...  10.4 us
    all_to_all x1, waiting for transfers between devices, per_device(): lax.all_to_all(my_rows, 'ch', split_axis=1, concat_axis=0, tiled=True)  9.4 us
    all_to_all x1, starting transfers between devices, per_device(): lax.all_to_all(my_rows, 'ch', split_axis=1, concat_axis=0, tiled=True)  7.39 us
  transfers between devices with their start and end apart: 3, of which 3 were waited for; matrix products, arithmetic and copies ran while one was open for 1% of the time, Pallas kernels for 0%

commit v1 on v0

--- a/solution.py
+++ b/solution.py
@@ -8,7 +8,7 @@
 
 def spread_2(block, axis, holder):
     block = jnp.where(lax.axis_index(axis) == holder, block, jnp.zeros_like(block))
-    return lax.psum(block, axis)
+    return jnp.sum(lax.all_gather(block, axis), axis=0)
 
 
 def detrend_cols(series):

time: 273 us -> 259 us (0.949)
  waiting for transfers between devices: 131 us -> 39.8 us
  blocking collectives: 0 us -> 79.4 us
    psum x1 -> x0, waiting for transfers between devices: 88.2 us -> none  [spread_2(): return lax.psum(block, axis)]
    all_gather x0 -> x4, blocking collectives: none -> 79.4 us  [spread_2(): return jnp.sum(lax.all_gather(block, axis), axis=0)]
    reduce_scatter x1, waiting for transfers between devices: 33.8 us -> 30.4 us  [per_device(): lax.psum_scatter(running.reshape(lag_count, c_dev, width_ref), 'seg', sca...]
  transfers between devices with their start and end apart: 3 -> 2, of which waited for: 3 -> 2; matrix products, arithmetic and copies ran while one was open for 1% -> 1% of each run, Pallas kernels for 0% -> 0%
where the time goes in v1:
time: 259 us
  local copies, waits for them, and re-layouts  102 us (39%)
  blocking collectives  79.4 us (31%)
  waiting for transfers between devices  39.8 us (15%)
  between operations  16.1 us (6%)
  matrix products  10.4 us (4%)
  starting transfers between devices  7.43 us (3%)
  other arithmetic  4.05 us (2%)
    while x126, local copies, waits for them, and re-layouts  89.3 us
    all_gather x4, blocking collectives, spread_2(): return jnp.sum(lax.all_gather(block, axis), axis=0)  79.4 us
    reduce_scatter x1, waiting for transfers between devices, per_device(): lax.psum_scatter(running.reshape(lag_count, c_dev, width_ref), 'seg', sca...  30.4 us
    dot_general x2, matrix products, add_block(): lax.dot_general(lagged, ref_block, (((0,), (0,)), ((), ())), preferred_el...  10.4 us
    all_to_all x1, waiting for transfers between devices, per_device(): lax.all_to_all(my_rows, 'ch', split_axis=1, concat_axis=0, tiled=True)  9.29 us
    all_to_all x1, starting transfers between devices, per_device(): lax.all_to_all(my_rows, 'ch', split_axis=1, concat_axis=0, tiled=True)  7.39 us
  transfers between devices with their start and end apart: 2, of which 2 were waited for; matrix products, arithmetic and copies ran while one was open for 1% of the time, Pallas kernels for 0%

profile of v1, /device:TPU:0, one launch (start us, length us, event | category | flops | bytes accessed | tf_op | source)
XLA Modules:
  0.0 258.8 jit_solution(3589788281017669755)
XLA Ops:
  6.5 1.1 copy.20
  7.7 1.0 copy.13
  8.6 7.4 %all-to-all-start = ((f32[64,16,128]{2,0,1:T(8,128)}), f32[64,16,128]{2,0,1:T(8,128)S(1)}, u32[]{:S(2)}, u32[]{:S(2)}) async-start(f32[64,16,128]{2,0,1:T(8,128)} %copy.13), calls=%async_computation | async-start | bytes 1048576 | tf_op jit(solution)/shard_map/all_to_all | solution.py:39
  16.1 1.5 fusion.3
  20.1 0.8 compare_and_fusion.3
  21.0 9.3 %all-to-all-done = f32[64,16,128]{2,0,1:T(8,128)S(1)} async-done(((f32[64,16,128]{2,0,1:T(8,128)}), f32[64,16,128]{2,0,1:T(8,128)S(1)}, u32[]{:S(2)}, u32[]{:S(2)}) %all-to-all-start) | async-done | bytes 524320 | tf_op jit(solution)/shard_map/all_to_all | solution.py:39
  31.9 21.3 %all-gather.3 = bf16[16384,16]{0,1:T(8,128)(2,1)S(1)} all-gather(bf16[1024,16]{0,1:T(8,128)(2,1)S(1)} %bitcast_select_fusion), channel_id=5, replica_groups=mesh['seg'=2,'ch'=16] {'ch'}, dimensions={0}, use_global_device_ids=true | all-gather | bytes 557056 | tf_op jit(solution)/shard_map/all_gather | solution.py:11
  54.4 18.9 %all-gather.2 = bf16[16384,16]{0,1:T(8,128)(2,1)S(1)} all-gather(bf16[1024,16]{0,1:T(8,128)(2,1)S(1)} %bitcast_select_fusion.1), channel_id=4, replica_groups=mesh['seg'=2,'ch'=16] {'ch'}, dimensions={0}, use_global_device_ids=true | all-gather | bytes 557056 | tf_op jit(solution)/shard_map/all_gather | solution.py:11
  74.4 20.4 %all-gather.1 = bf16[16384,16]{0,1:T(8,128)(2,1)S(1)} all-gather(bf16[1024,16]{0,1:T(8,128)(2,1)S(1)} %bitcast_select_fusion.2), channel_id=3, replica_groups=mesh['seg'=2,'ch'=16] {'ch'}, dimensions={0}, use_global_device_ids=true | all-gather | bytes 557056 | tf_op jit(solution)/shard_map/all_gather | solution.py:11
  96.0 18.9 %all-gather = bf16[16384,16]{0,1:T(8,128)(2,1)S(1)} all-gather(bf16[1024,16]{0,1:T(8,128)(2,1)S(1)} %bitcast_select_fusion.3), channel_id=2, replica_groups=mesh['seg'=2,'ch'=16] {'ch'}, dimensions={0}, use_global_device_ids=true | all-gather | bytes 557056 | tf_op jit(solution)/shard_map/all_gather | solution.py:11
  115.4 101.3 %while.14 = (s32[]{:T(128)}, f32[8192,64]{0,1:T(8,128)S(1)}, bf16[1088,128]{1,0:T(8,128)(2,1)S(1)}, bf16[1024,64]{0,1:T(8,128)(2,1)S(1)}, s32[]{:T(128)}, /*inde...) while((s32[]{:T(128)}, f32[8192,64]{0,1:T(8,128)S(1)}, ...), condition=%wide.region_7.9_spmd.clone, body=%wide.region_6.8_spmd.clone.sunk | while | flops 537919552 | bytes 29427356 | solution.py:61
  120.5 0.8 constant_dynamic-update-slice_fusion.135
  123.3 0.8 constant_dynamic-update-slice_fusion.139
  136.2 0.8 constant_dynamic-update-slice_fusion.157
  160.9 5.2 %convolution_add_fusion.2 = f32[8192,64]{0,1:T(8,128)S(1)} fusion(bf16[512,8192]{1,0:T(8,128)(2,1)} %constant_dynamic-update-slice_fusion.191, f32[8192,64]{0,1:T(8,128)S(1)} %get-tuple-element.243, pred[]{:T(512)S(6)} %compare.4, bf16[1024,64]{0,1:T(8,128)(2,1)S(1)} %get-tuple-element.317, s32[]{:T(128)S(6)} %select_n.98), kind=kOutput, calls=%fused_computation.4.clone.1 | convolution fusion | flops 537919488 | bytes 12648453 | tf_op jit(solution)/shard_map/while/body/eval_jaxpr/dot_general | solution.py:56
  171.1 0.8 constant_dynamic-update-slice_fusion.135
  174.0 0.8 constant_dynamic-update-slice_fusion.139
  186.8 0.8 constant_dynamic-update-slice_fusion.157
  204.4 0.8 constant_dynamic-update-slice_fusion.182
  211.5 5.2 %convolution_add_fusion.2 = f32[8192,64]{0,1:T(8,128)S(1)} fusion(bf16[512,8192]{1,0:T(8,128)(2,1)} %constant_dynamic-update-slice_fusion.191, f32[8192,64]{0,1:T(8,128)S(1)} %get-tuple-element.243, pred[]{:T(512)S(6)} %compare.4, bf16[1024,64]{0,1:T(8,128)(2,1)S(1)} %get-tuple-element.317, s32[]{:T(128)S(6)} %select_n.98), kind=kOutput, calls=%fused_computation.4.clone.1 | convolution fusion | flops 537919488 | bytes 12648453 | tf_op jit(solution)/shard_map/while/body/eval_jaxpr/dot_general | solution.py:56
  216.7 1.7 copy.25
  218.5 30.4 %reduce-scatter.2.cloned.1.call-done = f32[32,128,64]{1,0,2:T(8,128)} async-done(((f32[64,128,64]{1,0,2:T(8,128)}), f32[32,128,64]{1,0,2:T(8,128)}) %reduce-scatter.2.cloned.1.call-update) | async-done | bytes 1048592 | tf_op jit(solution)/shard_map/reduce_scatter | solution.py:62
  248.9 1.4 broadcast_divide_fusion
  250.3 1.6 copy.17
  (155 shorter events, 91.2 us)
Async XLA Ops:
  8.6 21.7 %all-to-all-start = ((f32[64,16,128]{2,0,1:T(8,128)}), f32[64,16,128]{2,0,1:T(8,128)S(1)}, u32[]{:S(2)}, u32[]{:S(2)}) async-start(f32[64,16,128]{2,0,1:T(8,128)} %copy.13), calls=%async_computation | async-start | bytes 1048576 | tf_op jit(solution)/shard_map/all_to_all | solution.py:39
  16.0 232.9 %reduce-scatter.2.cloned.1.call-start = ((), (), s32[]{:S(2)}) async-start(), calls=%async_computation.2 | async-start | bytes 3145728 | tf_op jit(solution)/shard_map/reduce_scatter | solution.py:62
Sparse Core Ops, SparseCore 0:
  218.6 30.2 reduce-scatter.1

commit v2 on v0

--- a/solution.py
+++ b/solution.py
@@ -36,7 +36,10 @@
     n_seg = lax.axis_size("seg")
     n_total = s_dev * n_ch
     c_dev = chans // n_ch
-    series = lax.all_to_all(my_rows, "ch", split_axis=1, concat_axis=0, tiled=True)
+    series = jnp.concatenate(
+        lax.all_to_all(jnp.stack(jnp.split(my_rows, lax.axis_size("ch"), axis=1)), "ch", 0, 0),
+        axis=0,
+    )
     detrended = detrend_cols(series)
     panels = owner_panels(detrended, ref_local, owners)
     width_ref = panels.shape[1]

time: 273 us -> 293 us (1.073)
  local copies, waits for them, and re-layouts: 100 us -> 120 us
    unnamed x3 -> x17, local copies, waits for them, and re-layouts: 3 us -> 22.5 us
where the time goes in v2:
time: 293 us; the launch traced here: 292 us
  waiting for transfers between devices  131 us (45%)
  local copies, waits for them, and re-layouts  120 us (41%)
  between operations  16 us (5%)
  matrix products  10.4 us (4%)
  starting transfers between devices  7.47 us (3%)
  other arithmetic  6.21 us (2%)
    while x126, local copies, waits for them, and re-layouts  89.4 us
    psum x1, waiting for transfers between devices, spread_2(): return lax.psum(block, axis)  88.2 us
    reduce_scatter x1, waiting for transfers between devices, per_device(): lax.psum_scatter(running.reshape(lag_count, c_dev, width_ref), 'seg', sca...  33.8 us
    unnamed x17, local copies, waits for them, and re-layouts  22.5 us
    dot_general x2, matrix products, add_block(): lax.dot_general(lagged, ref_block, (((0,), (0,)), ((), ())), preferred_el...  10.4 us
    all_to_all x1, waiting for transfers between devices, per_device(): lax.all_to_all(jnp.stack(jnp.split(my_rows, lax.axis_size('ch'), axis=1))...  9.34 us
    all_to_all x1, starting transfers between devices, per_device(): lax.all_to_all(jnp.stack(jnp.split(my_rows, lax.axis_size('ch'), axis=1))...  7.39 us
  transfers between devices with their start and end apart: 3, of which 3 were waited for; matrix products, arithmetic and copies ran while one was open for 1% of the time, Pallas kernels for 0%

profile of v2, /device:TPU:0, one launch (start us, length us, event | category | flops | bytes accessed | tf_op | source)
XLA Modules:
  0.0 291.9 jit_solution(9256294774244423079)
XLA Ops:
  6.5 1.4 fusion.17
  7.9 1.4 fusion.16
  9.3 1.4 fusion.15
  10.7 1.4 fusion.14
  12.0 1.4 fusion.13
  13.4 1.4 fusion.12
  14.8 1.4 fusion.11
  16.2 1.4 fusion.10
  17.5 1.4 fusion.9
  18.9 1.4 fusion.8
  20.3 1.4 fusion.7
  23.0 1.4 fusion.5
  25.8 1.4 fusion.3
  28.5 7.4 %all-to-all-start = ((f32[16,64,128]{2,1,0:T(8,128)}), f32[16,64,128]{2,1,0:T(8,128)S(1)}, u32[]{:S(2)}, u32[]{:S(2)}) async-start(f32[16,64,128]{2,1,0:T(8,128)} %fusion.2), calls=%async_computation | async-start | bytes 1048576 | tf_op jit(solution)/shard_map/all_to_all | solution.py:40
  36.0 1.5 fusion.19
  40.8 9.3 %all-to-all-done = f32[16,64,128]{2,1,0:T(8,128)S(1)} async-done(((f32[16,64,128]{2,1,0:T(8,128)}), f32[16,64,128]{2,1,0:T(8,128)S(1)}, u32[]{:S(2)}, u32[]{:S(2)}) %all-to-all-start) | async-done | bytes 524320 | tf_op jit(solution)/shard_map/all_to_all | solution.py:40
  56.2 88.2 %all-reduce.4.cloned.1.call-done = (bf16[1024,16]{0,1:T(8,128)(2,1)}, bf16[1024,16]{0,1:T(8,128)(2,1)}, bf16[1024,16]{0,1:T(8,128)(2,1)}, bf16[1024,16]{0,1:T(8,128)(2,1)}) async-done(((bf16[1024,16]{0,1:T(8,128)(2,1)}, bf16[1024,16]{0,1:T(8,128)(2,1)}, bf16[1024,16]{0,1:T(8,128)(2,1)}, bf16[1024,16]{0,1:T(8,128)(2,1)}), (bf16[1024,16]{0,1:T(8,128)(2,1)}, bf16[1024,16]{0,1:T(8,128)(2,1)}, ...) | async-done | bytes 131088 | tf_op jit(solution)/shard_map/psum | solution.py:11
  145.2 101.3 %while.14 = (s32[]{:T(128)}, f32[8192,64]{0,1:T(8,128)S(1)}, bf16[1088,128]{1,0:T(8,128)(2,1)S(1)}, bf16[1024,64]{0,1:T(8,128)(2,1)S(1)}, s32[]{:T(128)}, /*inde...) while((s32[]{:T(128)}, f32[8192,64]{0,1:T(8,128)S(1)}, ...), condition=%wide.region_7.9_spmd.clone, body=%wide.region_6.8_spmd.clone.sunk | while | flops 537919552 | bytes 29427356 | solution.py:64
  190.6 5.2 %convolution_add_fusion.2 = f32[8192,64]{0,1:T(8,128)S(1)} fusion(bf16[512,8192]{1,0:T(8,128)(2,1)} %constant_dynamic-update-slice_fusion.191, f32[8192,64]{0,1:T(8,128)S(1)} %get-tuple-element.245, pred[]{:T(512)S(6)} %compare.4, bf16[1024,64]{0,1:T(8,128)(2,1)S(1)} %get-tuple-element.319, s32[]{:T(128)S(6)} %select_n.98), kind=kOutput, calls=%fused_computation.4.clone.1 | convolution fusion | flops 537919488 | bytes 12648453 | tf_op jit(solution)/shard_map/while/body/eval_jaxpr/dot_general | solution.py:59
  241.3 5.2 %convolution_add_fusion.2 = f32[8192,64]{0,1:T(8,128)S(1)} fusion(bf16[512,8192]{1,0:T(8,128)(2,1)} %constant_dynamic-update-slice_fusion.191, f32[8192,64]{0,1:T(8,128)S(1)} %get-tuple-element.245, pred[]{:T(512)S(6)} %compare.4, bf16[1024,64]{0,1:T(8,128)(2,1)S(1)} %get-tuple-element.319, s32[]{:T(128)S(6)} %select_n.98), kind=kOutput, calls=%fused_computation.4.clone.1 | convolution fusion | flops 537919488 | bytes 12648453 | tf_op jit(solution)/shard_map/while/body/eval_jaxpr/dot_general | solution.py:59
  246.5 1.7 copy.13
  248.2 33.8 %reduce-scatter.2.cloned.1.call-done = f32[32,128,64]{1,0,2:T(8,128)} async-done(((f32[64,128,64]{1,0,2:T(8,128)}), f32[32,128,64]{1,0,2:T(8,128)}) %reduce-scatter.2.cloned.1.call-update) | async-done | bytes 1048592 | tf_op jit(solution)/shard_map/reduce_scatter | solution.py:65
  282.1 1.4 broadcast_divide_fusion
  283.5 1.6 copy.10
  (157 shorter events, 102.6 us)
Async XLA Ops:
  28.5 21.7 %all-to-all-start = ((f32[16,64,128]{2,1,0:T(8,128)}), f32[16,64,128]{2,1,0:T(8,128)S(1)}, u32[]{:S(2)}, u32[]{:S(2)}) async-start(f32[16,64,128]{2,1,0:T(8,128)} %fusion.2), calls=%async_computation | async-start | bytes 1048576 | tf_op jit(solution)/shard_map/all_to_all | solution.py:40
  35.9 108.4 %all-reduce.4.cloned.1.call-start = ((), (), s32[]{:S(2)}) async-start(), calls=%async_computation.3 | async-start | bytes 262144 | tf_op jit(solution)/shard_map/psum | solution.py:11
  55.9 226.2 %reduce-scatter.2.cloned.1.call-start = ((), (), s32[]{:S(2)}) async-start(), calls=%async_computation.2 | async-start | bytes 3145728 | tf_op jit(solution)/shard_map/reduce_scatter | solution.py:65
Sparse Core Ops, SparseCore 0:
  56.0 88.2 all-reduce.3
  248.3 33.6 reduce-scatter.1
